TPU v7x, 256 devices: a whole 4x4x8 slice. The times are simulated.
256 devices in a mesh: sec: 64 (over y, z, core), reg: 4 (over x).
Axes of the slice: x: 4, y: 4, z: 8, core: 2. Of those that a mesh axis runs over, the one named last changes fastest.
Arguments:
- start_params: float32 [64, 4, 20, 128], P('sec', 'reg'), may hold values from -3 to 3
- right_side: float32 [64, 4, 20, 128], P('sec', 'reg'), may hold values from -40 to 40
- prior: float32 [64, 4, 20, 128], P('sec', 'reg'), may hold values from 0.1 to 1
- matches: bfloat16 [64, 4, 640, 4, 256], P('sec', 'reg'), may hold values from -1 to 1
- pair_first: int32 [64, 4, 640], P('sec', 'reg'), may hold values from 0 to 127, as said below
- pair_second: int32 [64, 4, 640], P('sec', 'reg'), may hold values from 0 to 415, as said below
- match_counts: int32 [64, 4, 640], P('sec', 'reg'), may hold values from 0 to 256, as said below
- send_lists: int32 [64, 4, 2, 16], P('sec', 'reg'), may hold values from 0 to 127, as said below
Outputs:
- solution: float32 [64, 4, 20, 128], P('sec', 'reg')
- residual: float32 [64, 4, 20, 128], P('sec', 'reg')
Inputs may be any that keep to these rules, and one draw needn't show every extreme that they name: Each tile is pair_first of exactly five pairs of its device, in a drawn order. `pair_second`: names a column of the extended field; blocks of neighbours outside the grid are never named; a pair with match count 0 names its own tile. `match_counts`: 0 marks an absent pair; every device has a pair with exactly 256 matches. `send_lists`: row 0 holds the tiles whose coefficients a region lends to the region below it, row 1 to the region above; each row has 16 distinct tiles and the rows are disjoint.
All inputs are finite; a program needn't handle non-finite values.
Results may differ from a plain program's by a relative error of at most 0.0003.
Values sent between devices are 32-bit elements; how exact they have to be, the bound alone decides.
A program may use at most 64 MiB of HBM per device.

v0:
```python
import math
import jax
import jax.numpy as jnp
from jax import lax
from jax.sharding import PartitionSpec as P

FULL_PRECISION = lax.Precision.HIGHEST


def shifted(array, axis, by):
    length = lax.axis_size(axis)
    pairs = [(i, i + by) for i in range(length) if 0 <= i + by < length]
    return lax.ppermute(array, axis, pairs)


def padded_2(array, sides, width):
    for axis, dim in sides:
        size, length = (lax.axis_size(axis), array.shape[dim])
        up = [(i, (i + 1) % size) for i in range(size - 1)]
        down = [(j, i) for i, j in up]
        last = lax.slice_in_dim(array, length - width, length, axis=dim)
        first = lax.slice_in_dim(array, 0, width, axis=dim)
        before = lax.ppermute(last, axis, up)
        after = lax.ppermute(first, axis, down)
        array = jnp.concatenate([before, array, after], axis=dim)
    return array


def monomials(across, upward):
    constant = jnp.ones_like(across)
    square_a = across * across
    square_b = upward * upward
    mixed = across * upward
    return jnp.stack(
        [
            constant,
            across,
            upward,
            square_a,
            mixed,
            square_b,
            square_a * across,
            square_a * upward,
            square_b * across,
            square_b * upward,
        ]
    )


def match_bases(count_blk, match_blk):
    points = match_blk.astype(jnp.float32)
    slots = points.shape[-1]
    basis_a = monomials(points[:, 0], points[:, 1])
    basis_b = monomials(points[:, 2], points[:, 3])
    weights = jnp.where(jnp.arange(slots)[None, :] < count_blk[:, None], 2.0 / slots, 0.0).astype(
        jnp.float32
    )
    return (basis_a, basis_b, weights)


def block_terms(extended, first_blk, second_blk, count_blk, match_blk):
    width = first_blk.shape[0]
    basis_a, basis_b, weights = match_bases(count_blk, match_blk)
    own = jnp.take(extended, first_blk, axis=1).reshape(2, 10, width)
    other = jnp.take(extended, second_blk, axis=1).reshape(2, 10, width)
    mismatch = (
        jnp.einsum("mpk,cmp->cpk", basis_a, own, precision=FULL_PRECISION)
        - jnp.einsum("mpk,cmp->cpk", basis_b, other, precision=FULL_PRECISION)
    ) * weights[None]
    to_own = jnp.einsum("mpk,cpk->cmp", basis_a, mismatch, precision=FULL_PRECISION).reshape(
        20, width
    )
    to_other = -jnp.einsum("mpk,cpk->cmp", basis_b, mismatch, precision=FULL_PRECISION).reshape(
        20, width
    )
    return (to_own, to_other)


def split_blocks(first, second, counts, matches):
    pairs = first.shape[0]
    block = math.gcd(pairs, 512)
    blocks = pairs // block
    slots = matches.shape[-1]
    return (
        first.reshape(blocks, block),
        second.reshape(blocks, block),
        counts.reshape(blocks, block),
        matches.reshape(blocks, block, 4, slots),
    )


def extend(params, send_lists):
    arrived = params
    taken = []
    for hop_index in range(2):
        arrived = shifted(arrived, "sec", 1)
        taken.append(arrived)
    near_params, far_params = (taken[0], taken[1])
    faces = jnp.stack(
        [jnp.take(params, send_lists[0], axis=1), jnp.take(params, send_lists[1], axis=1)]
    )
    padded = padded_2(faces, (("reg", 0),), 1)
    return jnp.concatenate([params, near_params, far_params, padded[0], padded[3]], axis=1)


def fold_back(products, tiles, rows, send_lists):
    local = products[:, :tiles]
    near_part = products[:, tiles : 2 * tiles]
    far_part = products[:, 2 * tiles : 3 * tiles]
    outgoing = far_part
    arrived = far_part
    for hop_index in range(2):
        arrived = shifted(outgoing, "sec", -1)
        outgoing = near_part + arrived
    local = local + arrived
    faces = jnp.stack([products[:, 3 * tiles : 3 * tiles + rows], products[:, 3 * tiles + rows :]])
    padded = padded_2(faces, (("reg", 0),), 1)
    local = local.at[:, send_lists[0]].add(padded[0])
    return local.at[:, send_lists[1]].add(padded[3])


def apply_normal(params, prior, first, second, counts, matches, send_lists):
    tiles = params.shape[1]
    rows = send_lists.shape[1]
    pairs = first.shape[0]
    extended = extend(params, send_lists)
    pieces = split_blocks(first, second, counts, matches)
    to_own, to_other = lax.map(
        lambda items: block_terms(extended, items[0], items[1], items[2], items[3]), pieces
    )
    to_own = jnp.moveaxis(to_own, 0, 1).reshape(20, pairs)
    to_other = jnp.moveaxis(to_other, 0, 1).reshape(20, pairs)
    products = jnp.zeros((20, extended.shape[1]), jnp.float32)
    products = products.at[:, first].add(to_own).at[:, second].add(to_other)
    return fold_back(products, tiles, rows, send_lists) + prior * params


def global_dot(value):
    return lax.psum(value, ("sec", "reg"))


def on_device(
    start_params, right_side, prior, matches, pair_first, pair_second, match_counts, send_lists
):
    params_start = start_params[0, 0]
    target = right_side[0, 0]
    damping = prior[0, 0]
    first = pair_first[0, 0]
    second = pair_second[0, 0]
    counts = match_counts[0, 0]
    points = matches[0, 0]
    border = send_lists[0, 0]

    def normal(field):
        return apply_normal(field, damping, first, second, counts, points, border)

    solution = params_start
    residual = target - normal(params_start)
    direction = residual
    norm_now = global_dot(jnp.sum(residual * residual))
    image = normal(direction)
    alpha = norm_now / global_dot(jnp.sum(direction * image))
    solution = solution + alpha * direction
    residual = residual - alpha * image
    return (solution[None, None], residual[None, None])


def solution(mesh):
    return jax.shard_map(
        on_device,
        mesh=mesh,
        in_specs=(
            P("sec", "reg", None, None),
            P("sec", "reg", None, None),
            P("sec", "reg", None, None),
            P("sec", "reg", None, None, None),
            P("sec", "reg", None),
            P("sec", "reg", None),
            P("sec", "reg", None),
            P("sec", "reg", None, None),
        ),
        out_specs=(P("sec", "reg", None, None), P("sec", "reg", None, None)),
        check_vma=False,
    )
```

profile of v0, /device:TPU:1, one launch (start us, length us, event | category | flops | bytes accessed | tf_op | source)
XLA Modules:
  0.0 497.0 jit_solution(6133939188612458602)
XLA Ops:
  1.4 4.9 collective-permute-start
  23.0 152.0 %while.24 = (s32[]{:T(128)}, f32[5,20,128]{2,1,0:T(8,128)}, f32[5,20,128]{2,1,0:T(8,128)}, s32[5,128]{1,0:T(8,128)S(1)}, f32[20,416]{0,1:T(8,128)}, /*index=5*/b...) while((s32[]{:T(128)}, f32[5,20,128]{2,1,0:T(8,128)}, ...), condition=%wide.region_1.4_spmd, body=%wide.region_0.3_spmd.sunk | while | flops 32287744 | bytes 16952436 | solution.py:128
  27.2 4.8 stack.53
  32.7 5.4 %stack.52 = f32[10,128,256]{2,0,1:T(8,128)} concatenate(f32[1,128,256]{2,0,1:T(1,128)S(1)} %broadcast.300, f32[1,128,256]{2,0,1:T(1,128)} %get-tuple-element.348, f32[1,128,256]{2,0,1:T(1,128)} %get-tuple-element.349, f32[1,128,256]{2,0,1:T(1,128)S(1)} %get-tuple-element.350, f32[1,128,256]{2,0,1:T(1,128)S(1)} %get-tuple-element.351, f32[1,128,256]{2,0,1:T(1,128)S(1)} %get-tuple-element.352, ...), dimensions={0} | concatenate | bytes 2621440 | tf_op jit(solution)/shard_map/while/body/eval_jaxpr/stack | solution.py:34
  49.3 3.4 convolution_bitcast_fusion.4
  57.6 4.8 stack.53
  63.1 5.4 %stack.52 = f32[10,128,256]{2,0,1:T(8,128)} concatenate(f32[1,128,256]{2,0,1:T(1,128)S(1)} %broadcast.300, f32[1,128,256]{2,0,1:T(1,128)} %get-tuple-element.348, f32[1,128,256]{2,0,1:T(1,128)} %get-tuple-element.349, f32[1,128,256]{2,0,1:T(1,128)S(1)} %get-tuple-element.350, f32[1,128,256]{2,0,1:T(1,128)S(1)} %get-tuple-element.351, f32[1,128,256]{2,0,1:T(1,128)S(1)} %get-tuple-element.352, ...), dimensions={0} | concatenate | bytes 2621440 | tf_op jit(solution)/shard_map/while/body/eval_jaxpr/stack | solution.py:34
  87.9 4.8 stack.53
  93.5 5.4 %stack.52 = f32[10,128,256]{2,0,1:T(8,128)} concatenate(f32[1,128,256]{2,0,1:T(1,128)S(1)} %broadcast.300, f32[1,128,256]{2,0,1:T(1,128)} %get-tuple-element.348, f32[1,128,256]{2,0,1:T(1,128)} %get-tuple-element.349, f32[1,128,256]{2,0,1:T(1,128)S(1)} %get-tuple-element.350, f32[1,128,256]{2,0,1:T(1,128)S(1)} %get-tuple-element.351, f32[1,128,256]{2,0,1:T(1,128)S(1)} %get-tuple-element.352, ...), dimensions={0} | concatenate | bytes 2621440 | tf_op jit(solution)/shard_map/while/body/eval_jaxpr/stack | solution.py:34
  118.3 4.8 stack.53
  123.9 5.4 %stack.52 = f32[10,128,256]{2,0,1:T(8,128)} concatenate(f32[1,128,256]{2,0,1:T(1,128)S(1)} %broadcast.300, f32[1,128,256]{2,0,1:T(1,128)} %get-tuple-element.348, f32[1,128,256]{2,0,1:T(1,128)} %get-tuple-element.349, f32[1,128,256]{2,0,1:T(1,128)S(1)} %get-tuple-element.350, f32[1,128,256]{2,0,1:T(1,128)S(1)} %get-tuple-element.351, f32[1,128,256]{2,0,1:T(1,128)S(1)} %get-tuple-element.352, ...), dimensions={0} | concatenate | bytes 2621440 | tf_op jit(solution)/shard_map/while/body/eval_jaxpr/stack | solution.py:34
  148.7 4.8 stack.53
  154.3 5.4 %stack.52 = f32[10,128,256]{2,0,1:T(8,128)} concatenate(f32[1,128,256]{2,0,1:T(1,128)S(1)} %broadcast.300, f32[1,128,256]{2,0,1:T(1,128)} %get-tuple-element.348, f32[1,128,256]{2,0,1:T(1,128)} %get-tuple-element.349, f32[1,128,256]{2,0,1:T(1,128)S(1)} %get-tuple-element.350, f32[1,128,256]{2,0,1:T(1,128)S(1)} %get-tuple-element.351, f32[1,128,256]{2,0,1:T(1,128)S(1)} %get-tuple-element.352, ...), dimensions={0} | concatenate | bytes 2621440 | tf_op jit(solution)/shard_map/while/body/eval_jaxpr/stack | solution.py:34
  177.2 6.4 %scatter_custom_fusion = f32[20,416]{0,1:T(8,128)S(1)} fusion(s32[640]{0:T(1024)} %fusion.40, f32[640,20]{1,0:T(8,128)S(1)} %copy.78, f32[]{:T(128)} %constant.56.clone.1), kind=kCustom, calls=%fused_computation.104 | custom fusion | flops 12800 | bytes 33792 | tf_op jit(solution)/shard_map/scatter-add | solution.py:134
  183.6 6.1 %scatter_fusion = f32[20,416]{0,1:T(8,128)S(1)} fusion(f32[20,416]{0,1:T(8,128)S(1)} %scatter_custom_fusion, s32[640]{0:T(1024)S(1)} %fusion.41, f32[640,20]{1,0:T(8,128)S(1)} %copy.80), kind=kCustom, calls=%fused_computation.9 | custom fusion | flops 12800 | bytes 156160 | tf_op jit(solution)/shard_map/scatter-add | solution.py:134
  197.2 4.3 collective-permute-start.6
  206.6 5.1 %collective-permute-start.8 = (f32[20,128]{0,1:T(8,128)S(1)}, f32[20,128]{0,1:T(8,128)S(1)}, u32[]{:S(2)}, u32[]{:S(2)}) collective-permute-start(f32[20,128]{0,1:T(8,128)S(1)} %bitcast_subtract_fusion), channel_id=1, source_target_pairs={{0,4},{4,8},{8,12},{12,16},{16,20},{20,24},{24,28},{28,32},{32,36}... | collective-permute-start | bytes 30728 | tf_op jit(solution)/shard_map/ppermute | solution.py:13
  225.3 152.0 %while.25 = (s32[]{:T(128)}, f32[5,20,128]{2,1,0:T(8,128)}, f32[5,20,128]{2,1,0:T(8,128)}, s32[5,128]{1,0:T(8,128)S(1)}, f32[20,416]{0,1:T(8,128)}, /*index=5*/b...) while((s32[]{:T(128)}, f32[5,20,128]{2,1,0:T(8,128)}, ...), condition=%wide.region_9.12_spmd, body=%wide.region_8.11_spmd.sunk | while | flops 32287744 | bytes 16952436 | solution.py:128
  229.5 4.8 stack.71
  235.1 5.4 %stack.70 = f32[10,128,256]{2,0,1:T(8,128)} concatenate(f32[1,128,256]{2,0,1:T(1,128)S(1)} %broadcast.309, f32[1,128,256]{2,0,1:T(1,128)} %get-tuple-element.377, f32[1,128,256]{2,0,1:T(1,128)} %get-tuple-element.378, f32[1,128,256]{2,0,1:T(1,128)S(1)} %get-tuple-element.379, f32[1,128,256]{2,0,1:T(1,128)S(1)} %get-tuple-element.380, f32[1,128,256]{2,0,1:T(1,128)S(1)} %get-tuple-element.381, ...), dimensions={0} | concatenate | bytes 2621440 | tf_op jit(solution)/shard_map/while/body/eval_jaxpr/stack | solution.py:34
  259.9 4.8 stack.71
  265.5 5.4 %stack.70 = f32[10,128,256]{2,0,1:T(8,128)} concatenate(f32[1,128,256]{2,0,1:T(1,128)S(1)} %broadcast.309, f32[1,128,256]{2,0,1:T(1,128)} %get-tuple-element.377, f32[1,128,256]{2,0,1:T(1,128)} %get-tuple-element.378, f32[1,128,256]{2,0,1:T(1,128)S(1)} %get-tuple-element.379, f32[1,128,256]{2,0,1:T(1,128)S(1)} %get-tuple-element.380, f32[1,128,256]{2,0,1:T(1,128)S(1)} %get-tuple-element.381, ...), dimensions={0} | concatenate | bytes 2621440 | tf_op jit(solution)/shard_map/while/body/eval_jaxpr/stack | solution.py:34
  290.3 4.8 stack.71
  295.9 5.4 %stack.70 = f32[10,128,256]{2,0,1:T(8,128)} concatenate(f32[1,128,256]{2,0,1:T(1,128)S(1)} %broadcast.309, f32[1,128,256]{2,0,1:T(1,128)} %get-tuple-element.377, f32[1,128,256]{2,0,1:T(1,128)} %get-tuple-element.378, f32[1,128,256]{2,0,1:T(1,128)S(1)} %get-tuple-element.379, f32[1,128,256]{2,0,1:T(1,128)S(1)} %get-tuple-element.380, f32[1,128,256]{2,0,1:T(1,128)S(1)} %get-tuple-element.381, ...), dimensions={0} | concatenate | bytes 2621440 | tf_op jit(solution)/shard_map/while/body/eval_jaxpr/stack | solution.py:34
  320.7 4.8 stack.71
  326.2 5.4 %stack.70 = f32[10,128,256]{2,0,1:T(8,128)} concatenate(f32[1,128,256]{2,0,1:T(1,128)S(1)} %broadcast.309, f32[1,128,256]{2,0,1:T(1,128)} %get-tuple-element.377, f32[1,128,256]{2,0,1:T(1,128)} %get-tuple-element.378, f32[1,128,256]{2,0,1:T(1,128)S(1)} %get-tuple-element.379, f32[1,128,256]{2,0,1:T(1,128)S(1)} %get-tuple-element.380, f32[1,128,256]{2,0,1:T(1,128)S(1)} %get-tuple-element.381, ...), dimensions={0} | concatenate | bytes 2621440 | tf_op jit(solution)/shard_map/while/body/eval_jaxpr/stack | solution.py:34
  351.0 4.8 stack.71
  356.6 5.4 %stack.70 = f32[10,128,256]{2,0,1:T(8,128)} concatenate(f32[1,128,256]{2,0,1:T(1,128)S(1)} %broadcast.309, f32[1,128,256]{2,0,1:T(1,128)} %get-tuple-element.377, f32[1,128,256]{2,0,1:T(1,128)} %get-tuple-element.378, f32[1,128,256]{2,0,1:T(1,128)S(1)} %get-tuple-element.379, f32[1,128,256]{2,0,1:T(1,128)S(1)} %get-tuple-element.380, f32[1,128,256]{2,0,1:T(1,128)S(1)} %get-tuple-element.381, ...), dimensions={0} | concatenate | bytes 2621440 | tf_op jit(solution)/shard_map/while/body/eval_jaxpr/stack | solution.py:34
  379.5 6.4 %scatter_custom_fusion.4 = f32[20,416]{0,1:T(8,128)S(1)} fusion(s32[640]{0:T(1024)} %fusion.40, f32[640,20]{1,0:T(8,128)S(1)} %copy.89, f32[]{:T(128)} %constant.56.clone.1), kind=kCustom, calls=%fused_computation.102 | custom fusion | flops 12800 | bytes 33792 | tf_op jit(solution)/shard_map/scatter-add | solution.py:134
  385.9 6.1 %scatter_fusion.1 = f32[20,416]{0,1:T(8,128)S(1)} fusion(f32[20,416]{0,1:T(8,128)S(1)} %scatter_custom_fusion.4, s32[640]{0:T(1024)S(1)} %fusion.41, f32[640,20]{1,0:T(8,128)S(1)} %copy.91), kind=kCustom, calls=%fused_computation.13 | custom fusion | flops 12800 | bytes 156160 | tf_op jit(solution)/shard_map/scatter-add | solution.py:134
  395.3 3.5 collective-permute-done.12
  409.4 84.8 %all-reduce = (f32[]{:T(128)}, f32[]{:T(128)}) all-reduce(f32[]{:T(128)} %get-tuple-element.119, f32[]{:T(128)} %get-tuple-element.118), channel_id=1, replica_groups=mesh['sec'=64,'reg'=4] {'sec','reg'}, use_global_device_ids=true, to_apply=%region_7.10 | all-reduce | flops 2 | bytes 16 | tf_op jit(solution)/shard_map/psum | solution.py:139
  (392 shorter events, 259.9 us)
Async XLA Ops:
  1.4 21.6 %copy-start.2 = (f32[1,1,20,128]{2,3,1,0:T(8,128)}, f32[1,1,20,128]{2,3,1,0:T(8,128)S(1)}, u32[]{:S(2)}) copy-start(f32[1,1,20,128]{2,3,1,0:T(8,128)S(1)} %copy.69) | copy-start | bytes 30724
  1.4 12.7 %collective-permute-start = (f32[20,128]{0,1:T(8,128)S(1)}, f32[20,128]{0,1:T(8,128)S(1)}, u32[]{:S(2)}, u32[]{:S(2)}) collective-permute-start(f32[20,128]{0,1:T(8,128)S(1)} %bitcast.359), channel_id=1, source_target_pairs={{0,4},{4,8},{8,12},{12,16},{16,20},{20,24},{24,28},{28,32},{32,36}... | collective-permute-start | bytes 30728 | tf_op jit(solution)/shard_map/ppermute | solution.py:13
  7.1 13.3 %copy-start.10 = (pred[16]{0:T(512)(128)(4,1)}, pred[16]{0:T(512)(128)(4,1)S(1)}, u32[]{:S(2)}) copy-start(pred[16]{0:T(512)(128)(4,1)S(1)} %get-tuple-element.162) | copy-start | bytes 52
  7.8 12.7 %collective-permute-start.2 = (f32[1,20,16]{1,2,0:T(8,128)S(1)}, f32[1,20,16]{1,2,0:T(8,128)S(1)}, u32[]{:S(2)}, u32[]{:S(2)}) collective-permute-start(f32[1,20,16]{1,2,0:T(8,128)S(1)} %select_bitcast_fusion.7), channel_id=1, source_target_pairs={{0,1},{1,2},{2,3},{4,5},{5,6},{6,7},{8,9},{9,10},{10,11},{12,13},{... | collective-permute-start | bytes 3848 | tf_op jit(solution)/shard_map/ppermute | solution.py:23
  10.9 9.6 %copy-start.9 = (s32[1024]{0:T(1024)}, s32[1024]{0:T(1024)S(1)}, u32[]{:S(2)}) copy-start(s32[1024]{0:T(1024)S(1)} %pad_clamp_fusion.4) | copy-start | bytes 12292
  11.6 9.0 %collective-permute-start.3 = (f32[1,20,16]{1,2,0:T(8,128)S(1)}, f32[1,20,16]{1,2,0:T(8,128)S(1)}, u32[]{:S(2)}, u32[]{:S(2)}) collective-permute-start(f32[1,20,16]{1,2,0:T(8,128)S(1)} %select_bitcast_fusion.6), channel_id=1, source_target_pairs={{1,0},{2,1},{3,2},{5,4},{6,5},{7,6},{9,8},{10,9},{11,10},{13,12},{... | collective-permute-start | bytes 3848 | tf_op jit(solution)/shard_map/ppermute | solution.py:24
  14.2 6.5 %collective-permute-start.1 = (f32[20,128]{0,1:T(8,128)S(1)}, f32[20,128]{0,1:T(8,128)S(1)}, u32[]{:S(2)}, u32[]{:S(2)}) collective-permute-start(f32[20,128]{0,1:T(8,128)S(1)} %collective-permute-done), channel_id=1, source_target_pairs={{0,4},{4,8},{8,12},{12,16},{16,20},{20,24},{24,28},{28,32},{32,36}... | collective-permute-start | bytes 30728 | tf_op jit(solution)/shard_map/ppermute | solution.py:13
  175.0 16.9 %copy-start.14 = (s32[1,1,2,16]{3,2,1,0:T(2,128)S(1)}, s32[1,1,2,16]{3,2,1,0:T(2,128)}, u32[]{:S(2)}) copy-start(s32[1,1,2,16]{3,2,1,0:T(2,128)} %param.23) | copy-start | bytes 388
  175.0 16.9 %copy-start.7 = (f32[1,1,20,128]{3,1,2,0:T(1,128)S(1)}, f32[1,1,20,128]{3,1,2,0:T(1,128)}, u32[]{:S(2)}) copy-start(f32[1,1,20,128]{3,1,2,0:T(1,128)} %param.18) | copy-start | bytes 30724
  175.0 17.0 %copy-start.8 = (f32[1,1,20,128]{3,1,2,0:T(1,128)S(1)}, f32[1,1,20,128]{3,1,2,0:T(1,128)}, u32[]{:S(2)}) copy-start(f32[1,1,20,128]{3,1,2,0:T(1,128)} %param.17) | copy-start | bytes 30724
  175.0 27.8 %copy-start.3 = (f32[1,1,20,128]{2,3,1,0:T(8,128)S(1)}, f32[1,1,20,128]{2,3,1,0:T(8,128)}, u32[]{:S(2)}) copy-start(f32[1,1,20,128]{2,3,1,0:T(8,128)} %copy-done.2) | copy-start | bytes 30724
  175.9 36.4 %copy-start.13 = (pred[16]{0:T(512)(128)(4,1)S(1)}, pred[16]{0:T(512)(128)(4,1)}, u32[]{:S(2)}) copy-start(pred[16]{0:T(512)(128)(4,1)} %copy-done.12) | copy-start | bytes 52
  175.9 42.5 %copy-start.11 = (pred[16]{0:T(512)(128)(4,1)S(1)}, pred[16]{0:T(512)(128)(4,1)}, u32[]{:S(2)}) copy-start(pred[16]{0:T(512)(128)(4,1)} %copy-done.10) | copy-start | bytes 52
  189.7 5.6 %collective-permute-start.4 = (f32[20,128]{0,1:T(8,128)S(1)}, f32[20,128]{0,1:T(8,128)S(1)}, u32[]{:S(2)}, u32[]{:S(2)}) collective-permute-start(f32[20,128]{0,1:T(8,128)S(1)} %slice.106), channel_id=1, source_target_pairs={{4,0},{8,4},{12,8},{16,12},{20,16},{24,20},{28,24},{32,28},{36,32}... | collective-permute-start | bytes 30728 | tf_op jit(solution)/shard_map/ppermute | solution.py:13
  191.9 33.4 %copy-start.15 = (s32[16]{0:T(128)}, s32[16]{0:T(128)S(1)}, u32[]{:S(2)}) copy-start(s32[16]{0:T(128)S(1)} %get-tuple-element.210) | copy-start | bytes 196
  191.9 33.4 %copy-start.16 = (s32[16]{0:T(128)}, s32[16]{0:T(128)S(1)}, u32[]{:S(2)}) copy-start(s32[16]{0:T(128)S(1)} %get-tuple-element.211) | copy-start | bytes 196
  192.0 33.3 %copy-start.5 = (f32[1,1,20,128]{2,3,1,0:T(8,128)}, f32[1,1,20,128]{2,3,1,0:T(8,128)S(1)}, u32[]{:S(2)}) copy-start(f32[1,1,20,128]{2,3,1,0:T(8,128)S(1)} %copy.81) | copy-start | bytes 30724
  195.3 7.5 %collective-permute-start.5 = (f32[20,128]{0,1:T(8,128)S(1)}, f32[20,128]{0,1:T(8,128)S(1)}, u32[]{:S(2)}, u32[]{:S(2)}) collective-permute-start(f32[20,128]{0,1:T(8,128)S(1)} %slice_add_fusion.2), channel_id=1, source_target_pairs={{4,0},{8,4},{12,8},{16,12},{20,16},{24,20},{28,24},{32,28},{36,32}... | collective-permute-start | bytes 30728 | tf_op jit(solution)/shard_map/ppermute | solution.py:13
  197.2 5.6 %collective-permute-start.6 = (f32[1,20,16]{1,2,0:T(8,128)S(1)}, f32[1,20,16]{1,2,0:T(8,128)S(1)}, u32[]{:S(2)}, u32[]{:S(2)}) collective-permute-start(f32[1,20,16]{1,2,0:T(8,128)S(1)} %get-tuple-element.207), channel_id=1, source_target_pairs={{0,1},{1,2},{2,3},{4,5},{5,6},{6,7},{8,9},{9,10},{10,11},{12,13},{... | collective-permute-start | bytes 3848 | tf_op jit(solution)/shard_map/ppermute | solution.py:23
  201.5 4.4 collective-permute-start.7
  206.6 18.7 %copy-start = (f32[20,128]{0,1:T(8,128)}, f32[20,128]{0,1:T(8,128)S(1)}, u32[]{:S(2)}) copy-start(f32[20,128]{0,1:T(8,128)S(1)} %bitcast_subtract_fusion) | copy-start | bytes 30724
  206.6 9.5 %collective-permute-start.8 = (f32[20,128]{0,1:T(8,128)S(1)}, f32[20,128]{0,1:T(8,128)S(1)}, u32[]{:S(2)}, u32[]{:S(2)}) collective-permute-start(f32[20,128]{0,1:T(8,128)S(1)} %bitcast_subtract_fusion), channel_id=1, source_target_pairs={{0,4},{4,8},{8,12},{12,16},{16,20},{20,24},{24,28},{28,32},{32,36}... | collective-permute-start | bytes 30728 | tf_op jit(solution)/shard_map/ppermute | solution.py:13
  213.0 6.8 %collective-permute-start.10 = (f32[1,20,16]{1,2,0:T(8,128)S(1)}, f32[1,20,16]{1,2,0:T(8,128)S(1)}, u32[]{:S(2)}, u32[]{:S(2)}) collective-permute-start(f32[1,20,16]{1,2,0:T(8,128)S(1)} %select_bitcast_fusion.5), channel_id=1, source_target_pairs={{0,1},{1,2},{2,3},{4,5},{5,6},{6,7},{8,9},{9,10},{10,11},{12,13},{... | collective-permute-start | bytes 3848 | tf_op jit(solution)/shard_map/ppermute | solution.py:23
  216.2 6.8 %collective-permute-start.9 = (f32[20,128]{0,1:T(8,128)S(1)}, f32[20,128]{0,1:T(8,128)S(1)}, u32[]{:S(2)}, u32[]{:S(2)}) collective-permute-start(f32[20,128]{0,1:T(8,128)S(1)} %collective-permute-done.8), channel_id=1, source_target_pairs={{0,4},{4,8},{8,12},{12,16},{16,20},{20,24},{24,28},{28,32},{32,36}... | collective-permute-start | bytes 30728 | tf_op jit(solution)/shard_map/ppermute | solution.py:13
  218.5 4.4 collective-permute-start.11
  377.3 27.6 %copy-start.1 = (f32[20,128]{0,1:T(8,128)S(1)}, f32[20,128]{0,1:T(8,128)}, u32[]{:S(2)}) copy-start(f32[20,128]{0,1:T(8,128)} %copy-done) | copy-start | bytes 30724
  377.3 27.6 %copy-start.6 = (f32[1,1,20,128]{2,3,1,0:T(8,128)S(1)}, f32[1,1,20,128]{2,3,1,0:T(8,128)}, u32[]{:S(2)}) copy-start(f32[1,1,20,128]{2,3,1,0:T(8,128)} %copy-done.5) | copy-start | bytes 30724
  377.3 118.3 %copy-start.4 = (f32[1,1,20,128]{2,3,1,0:T(8,128)S(1)}, f32[1,1,20,128]{2,3,1,0:T(8,128)}, u32[]{:S(2)}) copy-start(f32[1,1,20,128]{2,3,1,0:T(8,128)} %copy-done.2) | copy-start | bytes 30724
  392.0 6.8 %collective-permute-start.12 = (f32[20,128]{0,1:T(8,128)S(1)}, f32[20,128]{0,1:T(8,128)S(1)}, u32[]{:S(2)}, u32[]{:S(2)}) collective-permute-start(f32[20,128]{0,1:T(8,128)S(1)} %slice.111), channel_id=1, source_target_pairs={{4,0},{8,4},{12,8},{16,12},{20,16},{24,20},{28,24},{32,28},{36,32}... | collective-permute-start | bytes 30728 | tf_op jit(solution)/shard_map/ppermute | solution.py:13
  398.8 6.1 %collective-permute-start.13 = (f32[20,128]{0,1:T(8,128)S(1)}, f32[20,128]{0,1:T(8,128)S(1)}, u32[]{:S(2)}, u32[]{:S(2)}) collective-permute-start(f32[20,128]{0,1:T(8,128)S(1)} %slice_add_fusion), channel_id=1, source_target_pairs={{4,0},{8,4},{12,8},{16,12},{20,16},{24,20},{28,24},{32,28},{36,32}... | collective-permute-start | bytes 30728 | tf_op jit(solution)/shard_map/ppermute | solution.py:13
  400.8 4.2 collective-permute-start.14
  403.6 4.4 collective-permute-start.15
  (1 other events, 3.8 us)
where the time goes:
time: 506 us; the launch traced here: 497 us
  local copies, waits for them, and re-layouts  185 us (37%)
  matrix products  93.3 us (18%)
  blocking collectives  84.8 us (17%)
  other arithmetic  74.4 us (15%)
  starting transfers between devices  42.1 us (8%)
  waiting for transfers between devices  14.2 us (3%)
    another operation x20, local copies, waits for them, and re-layouts, monomials(): jnp.stack([constant, across, upward, square_a, mixed, square_b, square_a...  102 us
    psum x1, blocking collectives, global_dot(): return lax.psum(value, ('sec', 'reg'))  84.8 us
    dot_general x10, matrix products, block_terms(): jnp.einsum('mpk,cpk->cmp', basis_a, mismatch, precision=FULL_PRECISION)  34.1 us
    dot_general x10, matrix products, block_terms(): jnp.einsum('mpk,cmp->cpk', basis_a, own, precision=FULL_PRECISION)  27.9 us
    scatter-add x4, other arithmetic, apply_normal(): products = products.at[:, first].add(to_own).at[:, second].add(to_other)  25 us
    ppermute x8, starting transfers between devices, shifted(): return lax.ppermute(array, axis, pairs)  23.6 us
    mul x10, other arithmetic, monomials(): square_b * upward  19.2 us
    dot_general x10, matrix products, block_terms(): jnp.einsum('mpk,cpk->cmp', basis_b, mismatch, precision=FULL_PRECISION)  18.3 us
  transfers between devices with their start and end apart: 16, of which 5 were waited for; matrix products, arithmetic and copies ran while one was open for 2% of the time, Pallas kernels for 0%

commit v1 on v0

--- a/solution.py
+++ b/solution.py
@@ -136,7 +136,10 @@
 
 
 def global_dot(value):
-    return lax.psum(value, ("sec", "reg"))
+    order_the_screen = lambda dev_axis, shard_axis, frame_in: lax.psum(
+        lax.psum(frame_in, dev_axis), shard_axis
+    )
+    return order_the_screen("reg", "sec", value)
 
 
 def on_device(

time: 506 us -> 558 us (1.10)
  blocking collectives: 84.8 us -> 137 us
    psum x1 -> x2, blocking collectives: 84.8 us -> 137 us  [the longest x1 130 us: global_dot(): lax.psum(lax.psum(frame_in, dev_axis), shard_axis)]
where the time goes in v1:
time: 558 us; the launch traced here: 549 us
  local copies, waits for them, and re-layouts  185 us (33%)
  blocking collectives  137 us (25%)
  matrix products  93.3 us (17%)
  other arithmetic  74.5 us (13%)
  starting transfers between devices  42.1 us (8%)
  waiting for transfers between devices  14.2 us (3%)
    psum x1, blocking collectives, global_dot(): lax.psum(lax.psum(frame_in, dev_axis), shard_axis)  130 us
    another operation x20, local copies, waits for them, and re-layouts, monomials(): jnp.stack([constant, across, upward, square_a, mixed, square_b, square_a...  102 us
    dot_general x10, matrix products, block_terms(): jnp.einsum('mpk,cpk->cmp', basis_a, mismatch, precision=FULL_PRECISION)  34.1 us
    dot_general x10, matrix products, block_terms(): jnp.einsum('mpk,cmp->cpk', basis_a, own, precision=FULL_PRECISION)  27.9 us
    scatter-add x4, other arithmetic, apply_normal(): products = products.at[:, first].add(to_own).at[:, second].add(to_other)  25 us
    ppermute x8, starting transfers between devices, shifted(): return lax.ppermute(array, axis, pairs)  23.6 us
    mul x10, other arithmetic, monomials(): square_b * upward  19.3 us
    dot_general x10, matrix products, block_terms(): jnp.einsum('mpk,cpk->cmp', basis_b, mismatch, precision=FULL_PRECISION)  18.3 us
  transfers between devices with their start and end apart: 16, of which 5 were waited for; matrix products, arithmetic and copies ran while one was open for 2% of the time, Pallas kernels for 0%

profile of v1, /device:TPU:1, one launch (start us, length us, event | category | flops | bytes accessed | tf_op | source)
XLA Modules:
  0.0 548.8 jit_solution(2430020261831072376)
XLA Ops:
  1.4 4.9 collective-permute-start
  23.0 152.0 %while.24 = (s32[]{:T(128)}, f32[5,20,128]{2,1,0:T(8,128)}, f32[5,20,128]{2,1,0:T(8,128)}, s32[5,128]{1,0:T(8,128)S(1)}, f32[20,416]{0,1:T(8,128)}, /*index=5*/b...) while((s32[]{:T(128)}, f32[5,20,128]{2,1,0:T(8,128)}, ...), condition=%wide.region_1.4_spmd, body=%wide.region_0.3_spmd.sunk | while | flops 32287744 | bytes 16952436 | solution.py:128
  27.2 4.8 stack.53
  32.8 5.4 stack.52
  57.6 4.8 stack.53
  63.2 5.4 stack.52
  88.0 4.8 stack.53
  93.6 5.4 stack.52
  118.4 4.8 stack.53
  124.0 5.4 stack.52
  148.8 4.8 stack.53
  154.3 5.4 stack.52
  177.2 6.4 %scatter_custom_fusion = f32[20,416]{0,1:T(8,128)S(1)} fusion(s32[640]{0:T(1024)} %fusion.40, f32[640,20]{1,0:T(8,128)S(1)} %copy.78, f32[]{:T(128)} %constant.56.clone.1), kind=kCustom, calls=%fused_computation.104 | custom fusion | flops 12800 | bytes 33792 | tf_op jit(solution)/shard_map/scatter-add | solution.py:134
  183.6 6.1 %scatter_fusion = f32[20,416]{0,1:T(8,128)S(1)} fusion(f32[20,416]{0,1:T(8,128)S(1)} %scatter_custom_fusion, s32[640]{0:T(1024)S(1)} %fusion.41, f32[640,20]{1,0:T(8,128)S(1)} %copy.80), kind=kCustom, calls=%fused_computation.9 | custom fusion | flops 12800 | bytes 156160 | tf_op jit(solution)/shard_map/scatter-add | solution.py:134
  197.3 4.3 collective-permute-start.6
  206.7 5.1 collective-permute-start.8
  225.3 152.0 %while.25 = (s32[]{:T(128)}, f32[5,20,128]{2,1,0:T(8,128)}, f32[5,20,128]{2,1,0:T(8,128)}, s32[5,128]{1,0:T(8,128)S(1)}, f32[20,416]{0,1:T(8,128)}, /*index=5*/b...) while((s32[]{:T(128)}, f32[5,20,128]{2,1,0:T(8,128)}, ...), condition=%wide.region_10.13_spmd, body=%wide.region_9.12_spmd.sunk | while | flops 32287744 | bytes 16952436 | solution.py:128
  229.5 4.8 stack.71
  235.1 5.4 stack.70
  259.9 4.8 stack.71
  265.5 5.4 stack.70
  290.3 4.8 stack.71
  295.9 5.4 stack.70
  320.7 4.8 stack.71
  326.3 5.4 stack.70
  351.1 4.8 stack.71
  356.7 5.4 stack.70
  379.5 6.4 %scatter_custom_fusion.4 = f32[20,416]{0,1:T(8,128)S(1)} fusion(s32[640]{0:T(1024)} %fusion.40, f32[640,20]{1,0:T(8,128)S(1)} %copy.89, f32[]{:T(128)} %constant.56.clone.1), kind=kCustom, calls=%fused_computation.102 | custom fusion | flops 12800 | bytes 33792 | tf_op jit(solution)/shard_map/scatter-add | solution.py:134
  385.9 6.1 %scatter_fusion.1 = f32[20,416]{0,1:T(8,128)S(1)} fusion(f32[20,416]{0,1:T(8,128)S(1)} %scatter_custom_fusion.4, s32[640]{0:T(1024)S(1)} %fusion.41, f32[640,20]{1,0:T(8,128)S(1)} %copy.91), kind=kCustom, calls=%fused_computation.13 | custom fusion | flops 12800 | bytes 156160 | tf_op jit(solution)/shard_map/scatter-add | solution.py:134
  395.3 3.5 collective-permute-done.12
  409.5 6.8 %all-reduce.1 = (f32[]{:T(128)}, f32[]{:T(128)}) all-reduce(f32[]{:T(128)} %get-tuple-element.119, f32[]{:T(128)} %get-tuple-element.118), channel_id=1, replica_groups=mesh['sec'=64,'reg'=4] {'reg'}, use_global_device_ids=true, to_apply=%region_7.10 | all-reduce | flops 2 | bytes 16 | tf_op jit(solution)/shard_map/psum | solution.py:140
  416.2 129.8 %all-reduce = (f32[]{:T(128)}, f32[]{:T(128)}) all-reduce(f32[]{:T(128)} %get-tuple-element.154, f32[]{:T(128)} %get-tuple-element.155), channel_id=1, replica_groups=mesh['sec'=64,'reg'=4] {'sec'}, use_global_device_ids=true, to_apply=%region_8.11 | all-reduce | flops 2 | bytes 16 | tf_op jit(solution)/shard_map/psum | solution.py:139
  (393 shorter events, 263.4 us)
Async XLA Ops:
  1.4 21.6 %copy-start.2 = (f32[1,1,20,128]{2,3,1,0:T(8,128)}, f32[1,1,20,128]{2,3,1,0:T(8,128)S(1)}, u32[]{:S(2)}) copy-start(f32[1,1,20,128]{2,3,1,0:T(8,128)S(1)} %copy.69) | copy-start | bytes 30724
  1.4 12.7 %collective-permute-start = (f32[20,128]{0,1:T(8,128)S(1)}, f32[20,128]{0,1:T(8,128)S(1)}, u32[]{:S(2)}, u32[]{:S(2)}) collective-permute-start(f32[20,128]{0,1:T(8,128)S(1)} %bitcast.359), channel_id=1, source_target_pairs={{0,4},{4,8},{8,12},{12,16},{16,20},{20,24},{24,28},{28,32},{32,36}... | collective-permute-start | bytes 30728 | tf_op jit(solution)/shard_map/ppermute | solution.py:13
  7.1 13.3 %copy-start.10 = (pred[16]{0:T(512)(128)(4,1)}, pred[16]{0:T(512)(128)(4,1)S(1)}, u32[]{:S(2)}) copy-start(pred[16]{0:T(512)(128)(4,1)S(1)} %get-tuple-element.164) | copy-start | bytes 52
  7.8 12.7 %collective-permute-start.2 = (f32[1,20,16]{1,2,0:T(8,128)S(1)}, f32[1,20,16]{1,2,0:T(8,128)S(1)}, u32[]{:S(2)}, u32[]{:S(2)}) collective-permute-start(f32[1,20,16]{1,2,0:T(8,128)S(1)} %select_bitcast_fusion.7), channel_id=1, source_target_pairs={{0,1},{1,2},{2,3},{4,5},{5,6},{6,7},{8,9},{9,10},{10,11},{12,13},{... | collective-permute-start | bytes 3848 | tf_op jit(solution)/shard_map/ppermute | solution.py:23
  10.9 9.6 %copy-start.9 = (s32[1024]{0:T(1024)}, s32[1024]{0:T(1024)S(1)}, u32[]{:S(2)}) copy-start(s32[1024]{0:T(1024)S(1)} %pad_clamp_fusion.4) | copy-start | bytes 12292
  11.6 9.0 %collective-permute-start.3 = (f32[1,20,16]{1,2,0:T(8,128)S(1)}, f32[1,20,16]{1,2,0:T(8,128)S(1)}, u32[]{:S(2)}, u32[]{:S(2)}) collective-permute-start(f32[1,20,16]{1,2,0:T(8,128)S(1)} %select_bitcast_fusion.6), channel_id=1, source_target_pairs={{1,0},{2,1},{3,2},{5,4},{6,5},{7,6},{9,8},{10,9},{11,10},{13,12},{... | collective-permute-start | bytes 3848 | tf_op jit(solution)/shard_map/ppermute | solution.py:24
  14.2 6.5 %collective-permute-start.1 = (f32[20,128]{0,1:T(8,128)S(1)}, f32[20,128]{0,1:T(8,128)S(1)}, u32[]{:S(2)}, u32[]{:S(2)}) collective-permute-start(f32[20,128]{0,1:T(8,128)S(1)} %collective-permute-done), channel_id=1, source_target_pairs={{0,4},{4,8},{8,12},{12,16},{16,20},{20,24},{24,28},{28,32},{32,36}... | collective-permute-start | bytes 30728 | tf_op jit(solution)/shard_map/ppermute | solution.py:13
  175.0 16.9 %copy-start.14 = (s32[1,1,2,16]{3,2,1,0:T(2,128)S(1)}, s32[1,1,2,16]{3,2,1,0:T(2,128)}, u32[]{:S(2)}) copy-start(s32[1,1,2,16]{3,2,1,0:T(2,128)} %param.23) | copy-start | bytes 388
  175.0 16.9 %copy-start.7 = (f32[1,1,20,128]{3,1,2,0:T(1,128)S(1)}, f32[1,1,20,128]{3,1,2,0:T(1,128)}, u32[]{:S(2)}) copy-start(f32[1,1,20,128]{3,1,2,0:T(1,128)} %param.18) | copy-start | bytes 30724
  175.0 17.0 %copy-start.8 = (f32[1,1,20,128]{3,1,2,0:T(1,128)S(1)}, f32[1,1,20,128]{3,1,2,0:T(1,128)}, u32[]{:S(2)}) copy-start(f32[1,1,20,128]{3,1,2,0:T(1,128)} %param.17) | copy-start | bytes 30724
  175.0 27.8 %copy-start.3 = (f32[1,1,20,128]{2,3,1,0:T(8,128)S(1)}, f32[1,1,20,128]{2,3,1,0:T(8,128)}, u32[]{:S(2)}) copy-start(f32[1,1,20,128]{2,3,1,0:T(8,128)} %copy-done.2) | copy-start | bytes 30724
  175.9 36.4 %copy-start.13 = (pred[16]{0:T(512)(128)(4,1)S(1)}, pred[16]{0:T(512)(128)(4,1)}, u32[]{:S(2)}) copy-start(pred[16]{0:T(512)(128)(4,1)} %copy-done.12) | copy-start | bytes 52
  175.9 42.5 %copy-start.11 = (pred[16]{0:T(512)(128)(4,1)S(1)}, pred[16]{0:T(512)(128)(4,1)}, u32[]{:S(2)}) copy-start(pred[16]{0:T(512)(128)(4,1)} %copy-done.10) | copy-start | bytes 52
  189.7 5.6 %collective-permute-start.4 = (f32[20,128]{0,1:T(8,128)S(1)}, f32[20,128]{0,1:T(8,128)S(1)}, u32[]{:S(2)}, u32[]{:S(2)}) collective-permute-start(f32[20,128]{0,1:T(8,128)S(1)} %slice.106), channel_id=1, source_target_pairs={{4,0},{8,4},{12,8},{16,12},{20,16},{24,20},{28,24},{32,28},{36,32}... | collective-permute-start | bytes 30728 | tf_op jit(solution)/shard_map/ppermute | solution.py:13
  191.9 33.4 %copy-start.15 = (s32[16]{0:T(128)}, s32[16]{0:T(128)S(1)}, u32[]{:S(2)}) copy-start(s32[16]{0:T(128)S(1)} %get-tuple-element.212) | copy-start | bytes 196
  191.9 33.4 %copy-start.16 = (s32[16]{0:T(128)}, s32[16]{0:T(128)S(1)}, u32[]{:S(2)}) copy-start(s32[16]{0:T(128)S(1)} %get-tuple-element.213) | copy-start | bytes 196
  192.0 33.3 %copy-start.5 = (f32[1,1,20,128]{2,3,1,0:T(8,128)}, f32[1,1,20,128]{2,3,1,0:T(8,128)S(1)}, u32[]{:S(2)}) copy-start(f32[1,1,20,128]{2,3,1,0:T(8,128)S(1)} %copy.81) | copy-start | bytes 30724
  195.3 7.5 %collective-permute-start.5 = (f32[20,128]{0,1:T(8,128)S(1)}, f32[20,128]{0,1:T(8,128)S(1)}, u32[]{:S(2)}, u32[]{:S(2)}) collective-permute-start(f32[20,128]{0,1:T(8,128)S(1)} %slice_add_fusion.2), channel_id=1, source_target_pairs={{4,0},{8,4},{12,8},{16,12},{20,16},{24,20},{28,24},{32,28},{36,32}... | collective-permute-start | bytes 30728 | tf_op jit(solution)/shard_map/ppermute | solution.py:13
  197.3 5.6 %collective-permute-start.6 = (f32[1,20,16]{1,2,0:T(8,128)S(1)}, f32[1,20,16]{1,2,0:T(8,128)S(1)}, u32[]{:S(2)}, u32[]{:S(2)}) collective-permute-start(f32[1,20,16]{1,2,0:T(8,128)S(1)} %get-tuple-element.209), channel_id=1, source_target_pairs={{0,1},{1,2},{2,3},{4,5},{5,6},{6,7},{8,9},{9,10},{10,11},{12,13},{... | collective-permute-start | bytes 3848 | tf_op jit(solution)/shard_map/ppermute | solution.py:23
  201.5 4.4 collective-permute-start.7
  206.6 18.7 %copy-start = (f32[20,128]{0,1:T(8,128)}, f32[20,128]{0,1:T(8,128)S(1)}, u32[]{:S(2)}) copy-start(f32[20,128]{0,1:T(8,128)S(1)} %bitcast_subtract_fusion) | copy-start | bytes 30724
  206.7 9.5 %collective-permute-start.8 = (f32[20,128]{0,1:T(8,128)S(1)}, f32[20,128]{0,1:T(8,128)S(1)}, u32[]{:S(2)}, u32[]{:S(2)}) collective-permute-start(f32[20,128]{0,1:T(8,128)S(1)} %bitcast_subtract_fusion), channel_id=1, source_target_pairs={{0,4},{4,8},{8,12},{12,16},{16,20},{20,24},{24,28},{28,32},{32,36}... | collective-permute-start | bytes 30728 | tf_op jit(solution)/shard_map/ppermute | solution.py:13
  213.1 6.8 %collective-permute-start.10 = (f32[1,20,16]{1,2,0:T(8,128)S(1)}, f32[1,20,16]{1,2,0:T(8,128)S(1)}, u32[]{:S(2)}, u32[]{:S(2)}) collective-permute-start(f32[1,20,16]{1,2,0:T(8,128)S(1)} %select_bitcast_fusion.5), channel_id=1, source_target_pairs={{0,1},{1,2},{2,3},{4,5},{5,6},{6,7},{8,9},{9,10},{10,11},{12,13},{... | collective-permute-start | bytes 3848 | tf_op jit(solution)/shard_map/ppermute | solution.py:23
  216.2 6.8 %collective-permute-start.9 = (f32[20,128]{0,1:T(8,128)S(1)}, f32[20,128]{0,1:T(8,128)S(1)}, u32[]{:S(2)}, u32[]{:S(2)}) collective-permute-start(f32[20,128]{0,1:T(8,128)S(1)} %collective-permute-done.8), channel_id=1, source_target_pairs={{0,4},{4,8},{8,12},{12,16},{16,20},{20,24},{24,28},{28,32},{32,36}... | collective-permute-start | bytes 30728 | tf_op jit(solution)/shard_map/ppermute | solution.py:13
  218.5 4.4 collective-permute-start.11
  377.3 27.6 %copy-start.1 = (f32[20,128]{0,1:T(8,128)S(1)}, f32[20,128]{0,1:T(8,128)}, u32[]{:S(2)}) copy-start(f32[20,128]{0,1:T(8,128)} %copy-done) | copy-start | bytes 30724
  377.3 27.6 %copy-start.6 = (f32[1,1,20,128]{2,3,1,0:T(8,128)S(1)}, f32[1,1,20,128]{2,3,1,0:T(8,128)}, u32[]{:S(2)}) copy-start(f32[1,1,20,128]{2,3,1,0:T(8,128)} %copy-done.5) | copy-start | bytes 30724
  377.3 170.0 %copy-start.4 = (f32[1,1,20,128]{2,3,1,0:T(8,128)S(1)}, f32[1,1,20,128]{2,3,1,0:T(8,128)}, u32[]{:S(2)}) copy-start(f32[1,1,20,128]{2,3,1,0:T(8,128)} %copy-done.2) | copy-start | bytes 30724
  392.1 6.8 %collective-permute-start.12 = (f32[20,128]{0,1:T(8,128)S(1)}, f32[20,128]{0,1:T(8,128)S(1)}, u32[]{:S(2)}, u32[]{:S(2)}) collective-permute-start(f32[20,128]{0,1:T(8,128)S(1)} %slice.111), channel_id=1, source_target_pairs={{4,0},{8,4},{12,8},{16,12},{20,16},{24,20},{28,24},{32,28},{36,32}... | collective-permute-start | bytes 30728 | tf_op jit(solution)/shard_map/ppermute | solution.py:13
  398.9 6.1 %collective-permute-start.13 = (f32[20,128]{0,1:T(8,128)S(1)}, f32[20,128]{0,1:T(8,128)S(1)}, u32[]{:S(2)}, u32[]{:S(2)}) collective-permute-start(f32[20,128]{0,1:T(8,128)S(1)} %slice_add_fusion), channel_id=1, source_target_pairs={{4,0},{8,4},{12,8},{16,12},{20,16},{24,20},{28,24},{32,28},{36,32}... | collective-permute-start | bytes 30728 | tf_op jit(solution)/shard_map/ppermute | solution.py:13
  400.8 4.2 collective-permute-start.14
  403.6 4.4 collective-permute-start.15
  (1 other events, 3.8 us)
